TPU v7x, 512 devices: a whole 4x8x8 slice. The times are simulated.
512 devices in a mesh: lat: 16 (over z, x_hi), lon: 32 (over y, x_lo, core).
Axes of the slice: x: 4 (x_hi: 2, x_lo: 2; x = x_hi * 2 + x_lo), y: 8, z: 8, core: 2. Of those that a mesh axis runs over, the one named last changes fastest.
Arguments:
- frame: bfloat16 [256, 512, 256], P('lat', 'lon'), may hold values from -64 to 64
- weight_qkv: bfloat16 [256, 768], replicated, may hold values from -0.375 to 0.375
- weight_proj: bfloat16 [256, 256], replicated, may hold values from -0.375 to 0.375
- gain_attn: float32 [256], replicated, may hold values from 0.5 to 1.5
- weight_up: bfloat16 [256, 1024], replicated, may hold values from -0.375 to 0.375
- weight_down: bfloat16 [1024, 256], replicated, may hold values from -0.1875 to 0.1875
- gain_mlp: float32 [256], replicated, may hold values from 0.5 to 1.5
- cotangent: bfloat16 [256, 512, 256], P('lat', 'lon'), may hold values from -6 to 6
Outputs:
- block_out: bfloat16 [256, 512, 256], P('lat', 'lon')
- grad_frame: bfloat16 [256, 512, 256], P('lat', 'lon')
- grad_qkv: bfloat16 [256, 768], replicated
- grad_proj: bfloat16 [256, 256], replicated
- grad_up: bfloat16 [256, 1024], replicated
- grad_down: bfloat16 [1024, 256], replicated
- grad_gain_attn: float32 [256], replicated
- grad_gain_mlp: float32 [256], replicated
All inputs are finite; a program needn't handle non-finite values.
Results may differ from a plain program's by a relative error of at most 0.012.
The roundings to bfloat16 on the way count: a program that leaves them out, or rounds other values in their place, can miss the bound.
Values may be sent and summed in bfloat16 or wider, within the bound.
No kernel may reach another device: no remote copies, remote signals or barrier semaphores. Data moves between devices by JAX's collectives and lax.ppermute only.
A program may use at most 128 MiB of HBM per device.

v0:
```python
import jax
import jax.numpy as jnp
from jax import lax
from jax.sharding import PartitionSpec as P

HEADS = 8
RADIUS = 6
epsilon = 1e-06
cubic_term = 0.044715
gelu_root = 0.7978845608028654
negative_big = -1e30


def padded_2(x, sides, width, wrap):
    for axis, dim in sides:
        devices, length = (lax.axis_size(axis), x.shape[dim])
        up = [(i, (i + 1) % devices) for i in range(devices if wrap else devices - 1)]
        down = [(j, i) for i, j in up]
        last = lax.slice_in_dim(x, length - width, length, axis=dim)
        first = lax.slice_in_dim(x, 0, width, axis=dim)
        before = lax.ppermute(last, axis, up)
        after = lax.ppermute(first, axis, down)
        x = jnp.concatenate([before, x, after], axis=dim)
    return x


def gelu_pair(upward):
    tangent = jnp.tanh(gelu_root * (upward + cubic_term * upward * upward * upward))
    activated = 0.5 * upward * (1.0 + tangent)
    derivative = 0.5 * (1.0 + tangent) + 0.5 * upward * (1.0 - tangent * tangent) * gelu_root * (
        1.0 + 3.0 * cubic_term * upward * upward
    )
    return (activated, derivative)


def rms_factor(field):
    return lax.rsqrt(jnp.mean(field * field, axis=-1, keepdims=True) + epsilon)


def norm_backward(incoming, field, factor):
    mean_term = jnp.mean(incoming * field, axis=-1, keepdims=True)
    return factor * (incoming - field * factor * factor * mean_term)


def contract_rows(left, right):
    return lax.dot_general(
        left, right, (((0,), (0,)), ((), ())), preferred_element_type=jnp.float32
    )


def contract_cols(left, right):
    return lax.dot_general(
        left, right, (((1,), (1,)), ((), ())), preferred_element_type=jnp.float32
    )


def row_strips(padded, rows, span):
    return jnp.stack(
        [lax.slice_in_dim(padded, offset, offset + rows, axis=0) for offset in range(span)], axis=1
    )


def unstrip(strip_sum, rows, span):
    total = jnp.zeros((rows + span - 1,) + strip_sum.shape[2:], strip_sum.dtype)
    for offset in range(span):
        total = total.at[offset : offset + rows].add(strip_sum[:, offset])
    return total


def fold_rims(field, axis, length, radius):
    middle = lax.slice_in_dim(field, 2 * radius, 2 * radius + length, axis=axis)
    front = lax.slice_in_dim(field, 0, radius, axis=axis)
    back = lax.slice_in_dim(field, length + 3 * radius, length + 4 * radius, axis=axis)
    widths_front = [(0, 0)] * field.ndim
    widths_front[axis] = (0, length - radius)
    widths_back = [(0, 0)] * field.ndim
    widths_back[axis] = (length - radius, 0)
    return middle + jnp.pad(front, widths_front) + jnp.pad(back, widths_back)


def band_strips(padded, rows, span, heads):
    strips = row_strips(padded, rows, span)
    return strips.reshape(rows, span * padded.shape[1], heads, padded.shape[2] // heads)


def on_device(
    frame, weight_qkv, weight_proj, gain_attn, weight_up, weight_down, gain_mlp, cotangent
):
    lat_rows, lon_cols, width = frame.shape
    heads = HEADS
    head_size = width // heads
    radius = RADIUS
    span = 2 * radius + 1
    head_scale = head_size ** (-0.5)
    pad_rows = lat_rows + 2 * radius
    pad_cols = lon_cols + 2 * radius
    band = span * pad_cols
    local_tokens = lat_rows * lon_cols
    lat_total = lat_rows * lax.axis_size("lat")
    tokens_all = lat_total * lon_cols * lax.axis_size("lon")
    grad_scale = tokens_all ** (-0.5)
    lat_first = lax.axis_index("lat") * lat_rows
    row_global = lat_first + jnp.arange(lat_rows)[:, None] + jnp.arange(span)[None, :] - radius
    row_ok = (row_global >= 0) & (row_global < lat_total)
    col_gap = jnp.arange(pad_cols)[None, :] - radius - jnp.arange(lon_cols)[:, None]
    near = jnp.abs(col_gap) <= radius
    valid = (row_ok[:, None, :, None] & near[None, :, None, :]).reshape(lat_rows, 1, lon_cols, band)
    flat = frame.reshape(local_tokens, width)
    projected = jnp.dot(flat, weight_qkv, preferred_element_type=jnp.float32).astype(jnp.bfloat16)
    queries = projected[:, :width]
    pairs = projected[:, width:].reshape(lat_rows, lon_cols, 2 * width)
    widened = padded_2(pairs, (("lon", 1),), radius, True)
    margined = padded_2(widened, (("lat", 0),), radius, False)
    pair_pad = margined.reshape(-1, 2 * width)
    queries4 = queries.reshape(lat_rows, lon_cols, heads, head_size)
    keys_pad = pair_pad[:, :width].reshape(pad_rows, pad_cols, width)
    values_pad = pair_pad[:, width:].reshape(pad_rows, pad_cols, width)
    key_strip = band_strips(keys_pad, lat_rows, span, heads)
    value_strip = band_strips(values_pad, lat_rows, span, heads)
    scores = (
        jnp.einsum("ichd,inhd->ihcn", queries4, key_strip, preferred_element_type=jnp.float32)
        * head_scale
    )
    scores = jnp.where(valid, scores, negative_big)
    peak = jnp.max(scores, axis=3, keepdims=True)
    expo = jnp.exp(scores - peak)
    total = jnp.sum(expo, axis=3, keepdims=True)
    probs = expo / total
    probs_bf = probs.astype(jnp.bfloat16)
    attended = (
        jnp.einsum("ihcn,inhd->ichd", probs_bf, value_strip, preferred_element_type=jnp.float32)
        .astype(jnp.bfloat16)
        .reshape(local_tokens, width)
    )
    proj = jnp.dot(attended, weight_proj, preferred_element_type=jnp.float32)
    factor_one = rms_factor(proj)
    mid = (flat.astype(jnp.float32) + proj * factor_one * gain_attn).astype(jnp.bfloat16)
    upward = jnp.dot(mid, weight_up, preferred_element_type=jnp.float32)
    activated, derivative = gelu_pair(upward)
    hidden = activated.astype(jnp.bfloat16)
    downward = jnp.dot(hidden, weight_down, preferred_element_type=jnp.float32)
    factor_two = rms_factor(downward)
    block_out = (mid.astype(jnp.float32) + downward * factor_two * gain_mlp).astype(jnp.bfloat16)
    incoming = cotangent.reshape(local_tokens, width).astype(jnp.float32)
    local_gain_mlp = jnp.sum(incoming * downward * factor_two, axis=0)
    d_down = norm_backward(incoming * gain_mlp, downward, factor_two).astype(jnp.bfloat16)
    local_down = contract_rows(hidden, d_down)
    d_up = (contract_cols(d_down, weight_down) * derivative).astype(jnp.bfloat16)
    local_up = contract_rows(mid, d_up)
    d_mid = incoming + contract_cols(d_up, weight_up)
    local_gain_attn = jnp.sum(d_mid * proj * factor_one, axis=0)
    d_proj = norm_backward(d_mid * gain_attn, proj, factor_one).astype(jnp.bfloat16)
    local_proj = contract_rows(attended, d_proj)
    d_attended = contract_cols(d_proj, weight_proj).astype(jnp.bfloat16)
    d_attended4 = d_attended.reshape(lat_rows, lon_cols, heads, head_size)
    d_probs = jnp.einsum(
        "ichd,inhd->ihcn", d_attended4, value_strip, preferred_element_type=jnp.float32
    )
    d_weighted = jnp.sum(probs * d_probs, axis=3, keepdims=True)
    d_scores = (probs * (d_probs - d_weighted) * head_scale).astype(jnp.bfloat16)
    d_queries = jnp.einsum(
        "ihcn,inhd->ichd", d_scores, key_strip, preferred_element_type=jnp.float32
    ).reshape(local_tokens, width)
    key_terms = jnp.einsum(
        "ihcn,ichd->inhd", d_scores, queries4, preferred_element_type=jnp.float32
    ).reshape(lat_rows, span, pad_cols, width)
    value_terms = jnp.einsum(
        "ihcn,ichd->inhd", probs_bf, d_attended4, preferred_element_type=jnp.float32
    ).reshape(lat_rows, span, pad_cols, width)
    pair_grads = unstrip(jnp.concatenate([key_terms, value_terms], axis=3), lat_rows, span)
    widened_grads = padded_2(pair_grads.astype(jnp.bfloat16), (("lon", 1),), radius, True).astype(
        pair_grads.dtype
    )
    margined_grads = padded_2(
        widened_grads.astype(jnp.bfloat16), (("lat", 0),), radius, False
    ).astype(widened_grads.dtype)
    owned = fold_rims(fold_rims(margined_grads, 0, lat_rows, radius), 1, lon_cols, radius).reshape(
        local_tokens, 2 * width
    )
    d_projected = jnp.concatenate([d_queries, owned], axis=1).astype(jnp.bfloat16)
    local_qkv = contract_rows(flat, d_projected)
    grad_frame = (d_mid + contract_cols(d_projected, weight_qkv)).astype(jnp.bfloat16)
    sum_qkv, sum_proj, sum_up, sum_down, sum_gain_attn, sum_gain_mlp = lax.psum(
        (local_qkv, local_proj, local_up, local_down, local_gain_attn, local_gain_mlp),
        ("lat", "lon"),
    )
    return (
        block_out.reshape(lat_rows, lon_cols, width),
        grad_frame.reshape(lat_rows, lon_cols, width),
        (sum_qkv * grad_scale).astype(jnp.bfloat16),
        (sum_proj * grad_scale).astype(jnp.bfloat16),
        (sum_up * grad_scale).astype(jnp.bfloat16),
        (sum_down * grad_scale).astype(jnp.bfloat16),
        sum_gain_attn * grad_scale,
        sum_gain_mlp * grad_scale,
    )


def solution(mesh):
    return jax.shard_map(
        on_device,
        mesh=mesh,
        in_specs=(P("lat", "lon", None), P(), P(), P(), P(), P(), P(), P("lat", "lon", None)),
        out_specs=(P("lat", "lon", None), P("lat", "lon", None), P(), P(), P(), P(), P(), P()),
        check_vma=False,
    )
```

profile of v0, /device:TPU:17, one launch (start us, length us, event | category | flops | bytes accessed | tf_op | source)
XLA Modules:
  0.0 695.6 jit_solution(14059497985502001922)
XLA Ops:
  8.7 3.7 collective-permute-start
  15.1 3.6 collective-permute-done.1
  18.8 4.4 collective-permute-start.2
  25.2 2.3 collective-permute-done.2
  27.4 5.3 collective-permute-done.3
  79.8 18.8 %copy.50 = bf16[16,13,28,256]{2,1,3,0:T(8,128)(2,1)} copy(bf16[16,13,28,256]{3,2,0,1:T(8,128)(2,1)} %constant_dynamic-update-slice_fusion.13) | data formatting | bytes 5963776 | tf_op jit(solution)/shard_map/reshape | solution.py:83
  98.6 21.2 %reshape.626 = bf16[16,364,8,32]{1,3,2,0:T(8,128)(2,1)} reshape(bf16[16,13,28,256]{2,1,3,0:T(8,128)(2,1)} %copy.50) | data formatting | bytes 5963776 | tf_op jit(solution)/shard_map/reshape | solution.py:83
  128.6 18.8 %copy.49 = bf16[16,13,28,256]{2,1,3,0:T(8,128)(2,1)} copy(bf16[16,13,28,256]{3,2,0,1:T(8,128)(2,1)} %constant_dynamic-update-slice_fusion) | data formatting | bytes 5963776 | tf_op jit(solution)/shard_map/reshape | solution.py:83
  147.4 21.2 %reshape.625 = bf16[16,364,8,32]{1,3,2,0:T(8,128)(2,1)} reshape(bf16[16,13,28,256]{2,1,3,0:T(8,128)(2,1)} %copy.49) | data formatting | bytes 5963776 | tf_op jit(solution)/shard_map/reshape | solution.py:83
  168.6 2.6 fusion.52
  171.2 3.8 fusion.78
  182.0 4.3 fusion.49
  186.3 17.5 %fusion.20 = bf16[16,16,8,32]{3,1,2,0:T(8,128)(2,1)} fusion(bf16[16,364,8,32]{1,3,2,0:T(8,128)(2,1)} %reshape.626, f32[16,8,16,364]{3,2,1,0:T(8,128)} %fusion.49, f32[16,8,16,364]{3,2,1,0:T(8,128)} %copy-done.5, f32[16,8,16]{2,1,0:T(8,128)S(1)} %get-tuple-element.226), kind=kOutput, calls=%fused_computation.27 | convolution fusion | flops 52996460 | bytes 9084928 | tf_op jit(solution)/shard_map/ihcn,inhd->ichd/dot_general | solution.py:161
  203.8 17.6 %convolution_bitcast_fusion.1 = f32[16,364,8,32]{1,3,2,0:T(8,128)} fusion(f32[16,8,16,364]{3,2,1,0:T(8,128)} %fusion.49, bf16[16,16,8,32]{3,2,1,0:T(8,128)(2,1)S(1)} %reshape.602, f32[16,8,16,364]{3,2,1,0:T(8,128)} %copy-done.5, f32[16,8,16]{2,1,0:T(8,128)S(1)} %get-tuple-element.226), kind=kOutput, calls=%fused_computation.8 | convolution fusion | flops 52930924 | bytes 12066816 | tf_op jit(solution)/shard_map/ihcn,ichd->inhd/dot_general | solution.py:164
  221.3 5.6 convolution_bitcast_fusion
  226.9 20.3 %copy.46 = f32[16,364,8,32]{3,2,0,1:T(8,128)} copy(f32[16,364,8,32]{1,3,2,0:T(8,128)} %convolution_bitcast_fusion) | data formatting | bytes 11927552 | tf_op jit(solution)/shard_map/ihcn,ichd->inhd/transpose | solution.py:167
  247.3 16.9 %reshape.609 = f32[16,13,28,256]{3,0,2,1:T(8,128)} reshape(f32[16,364,8,32]{3,2,0,1:T(8,128)} %copy.46) | data formatting | bytes 11927552 | tf_op jit(solution)/shard_map/reshape | solution.py:169
  264.2 20.3 %copy.44 = f32[16,364,8,32]{3,2,0,1:T(8,128)} copy(f32[16,364,8,32]{1,3,2,0:T(8,128)} %convolution_bitcast_fusion.1) | data formatting | bytes 11927552 | tf_op jit(solution)/shard_map/ihcn,ichd->inhd/transpose | solution.py:164
  284.5 16.8 %reshape.608 = f32[16,13,28,256]{3,0,2,1:T(8,128)} reshape(f32[16,364,8,32]{3,2,0,1:T(8,128)} %copy.44) | data formatting | bytes 11927552 | tf_op jit(solution)/shard_map/reshape | solution.py:166
  301.3 3.8 constant_dynamic-update-slice_fusion.27
  307.7 4.1 copy-done.2
  312.0 2.2 scatter-add.45
  338.8 2.5 scatter-add.59
  342.8 2.5 scatter-add.60
  346.7 2.5 scatter-add.61
  350.6 2.5 scatter-add.64
  355.3 3.2 collective-permute-start.5
  360.1 3.7 collective-permute-done.5
  364.8 5.1 collective-permute-start.6
  374.2 9.6 %collective-permute-done.6 = bf16[6,40,512]{2,0,1:T(8,128)(2,1)S(1)} collective-permute-done((bf16[6,40,512]{2,0,1:T(8,128)(2,1)}, bf16[6,40,512]{2,0,1:T(8,128)(2,1)S(1)}, u32[]{:S(2)}, u32[]{:S(2)}) %collective-permute-start.6) | collective-permute-done | bytes 245792 | tf_op jit(solution)/shard_map/ppermute | solution.py:21
  386.7 106.6 %all-reduce.3 = (f32[256]{0:T(256)S(1)}, f32[256]{0:T(256)S(1)}) all-reduce(f32[256]{0:T(256)S(1)} %get-tuple-element.180, f32[256]{0:T(256)S(1)} %get-tuple-element.182), channel_id=1, replica_groups=mesh['lat'=16,'lon'=32] {'lat','lon'}, use_global_device_ids=true, to_apply=%region_12.13 | all-reduce | flops 512 | bytes 4096 | tf_op jit(solution)/shard_map/psum | solution.py:183
  494.9 186.8 %all-reduce.7.cloned.1.call-done = (f32[256,768]{0,1:T(8,128)}, f32[256,256]{1,0:T(8,128)}, f32[256,1024]{1,0:T(8,128)}, f32[1024,256]{1,0:T(8,128)}) async-done(((f32[256,768]{0,1:T(8,128)}, f32[256,256]{1,0:T(8,128)}, f32[256,1024]{1,0:T(8,128)}, f32[1024,256]{1,0:T(8,128)}), (f32[256,768]{0,1:T(8,128)}, f32[256,256]{1,0:T(8,128)}, f32[256,1024]{1,0:T(8,128)}, ...) | async-done | bytes 3145744 | tf_op jit(solution)/shard_map/psum | solution.py:183
  (226 shorter events, 120.4 us)
Async XLA Ops:
  7.2 170.5 %copy-start = (bf16[256,1024]{1,0:T(8,128)(2,1)S(1)}, bf16[256,1024]{1,0:T(8,128)(2,1)}, u32[]{:S(2)}) copy-start(bf16[256,1024]{1,0:T(8,128)(2,1)} %param.38) | copy-start | bytes 1572868
  7.2 674.5 %all-reduce.7.cloned.1.call-start = ((), (), s32[]{:S(2)}) async-start(), calls=%async_computation | async-start | bytes 6291456 | tf_op jit(solution)/shard_map/psum | solution.py:183
  8.7 6.4 collective-permute-start
  12.4 6.3 collective-permute-start.1
  18.8 8.6 %collective-permute-start.2 = (bf16[6,28,512]{2,1,0:T(8,128)(2,1)S(1)}, bf16[6,28,512]{2,1,0:T(8,128)(2,1)S(1)}, u32[]{:S(2)}, u32[]{:S(2)}) collective-permute-start(bf16[6,28,512]{2,1,0:T(8,128)(2,1)S(1)} %get-tuple-element.220), channel_id=1, source_target_pairs={{0,32},{32,64},{64,96},{96,128},{128,160},{160,192},{192,224},{224... | collective-permute-start | bytes 516104 | tf_op jit(solution)/shard_map/ppermute | solution.py:21
  23.2 9.6 %collective-permute-start.3 = (bf16[6,28,512]{2,1,0:T(8,128)(2,1)S(1)}, bf16[6,28,512]{2,1,0:T(8,128)(2,1)S(1)}, u32[]{:S(2)}, u32[]{:S(2)}) collective-permute-start(bf16[6,28,512]{2,1,0:T(8,128)(2,1)S(1)} %get-tuple-element.221), channel_id=1, source_target_pairs={{32,0},{64,32},{96,64},{128,96},{160,128},{192,160},{224,192},{256... | collective-permute-start | bytes 516104 | tf_op jit(solution)/shard_map/ppermute | solution.py:22
  38.1 19.4 %copy-start.31 = (bf16[448,256]{1,0:T(8,128)(2,1)S(1)}, bf16[448,256]{1,0:T(8,128)(2,1)}, u32[]{:S(2)}) copy-start(bf16[448,256]{1,0:T(8,128)(2,1)} %get-tuple-element.206) | copy-start | bytes 688132
  38.1 20.1 %copy-start.30 = (bf16[448,256]{1,0:T(8,128)(2,1)S(1)}, bf16[448,256]{1,0:T(8,128)(2,1)}, u32[]{:S(2)}) copy-start(bf16[448,256]{1,0:T(8,128)(2,1)} %get-tuple-element.207) | copy-start | bytes 688132
  38.9 19.4 %copy-start.29 = (bf16[448,256]{1,0:T(8,128)(2,1)S(1)}, bf16[448,256]{1,0:T(8,128)(2,1)}, u32[]{:S(2)}) copy-start(bf16[448,256]{1,0:T(8,128)(2,1)} %get-tuple-element.208) | copy-start | bytes 688132
  64.5 10.2 %copy-start.26 = (bf16[16,1,28,256]{3,2,0,1:T(8,128)(2,1)S(1)}, bf16[16,1,28,256]{3,2,0,1:T(8,128)(2,1)}, u32[]{:S(2)}) copy-start(bf16[16,1,28,256]{3,2,0,1:T(8,128)(2,1)} %stack.104) | copy-start | bytes 688132
  64.5 10.9 %copy-start.25 = (bf16[16,1,28,256]{3,2,0,1:T(8,128)(2,1)S(1)}, bf16[16,1,28,256]{3,2,0,1:T(8,128)(2,1)}, u32[]{:S(2)}) copy-start(bf16[16,1,28,256]{3,2,0,1:T(8,128)(2,1)} %stack.105) | copy-start | bytes 688132
  64.5 11.7 %copy-start.24 = (bf16[16,1,28,256]{3,2,0,1:T(8,128)(2,1)S(1)}, bf16[16,1,28,256]{3,2,0,1:T(8,128)(2,1)}, u32[]{:S(2)}) copy-start(bf16[16,1,28,256]{3,2,0,1:T(8,128)(2,1)} %stack.106) | copy-start | bytes 688132
  64.5 12.4 %copy-start.23 = (bf16[16,1,28,256]{3,2,0,1:T(8,128)(2,1)S(1)}, bf16[16,1,28,256]{3,2,0,1:T(8,128)(2,1)}, u32[]{:S(2)}) copy-start(bf16[16,1,28,256]{3,2,0,1:T(8,128)(2,1)} %stack.107) | copy-start | bytes 688132
  64.5 13.1 %copy-start.21 = (bf16[16,1,28,256]{3,2,0,1:T(8,128)(2,1)S(1)}, bf16[16,1,28,256]{3,2,0,1:T(8,128)(2,1)}, u32[]{:S(2)}) copy-start(bf16[16,1,28,256]{3,2,0,1:T(8,128)(2,1)} %stack.108) | copy-start | bytes 688132
  64.5 13.9 %copy-start.19 = (bf16[16,1,28,256]{3,2,0,1:T(8,128)(2,1)S(1)}, bf16[16,1,28,256]{3,2,0,1:T(8,128)(2,1)}, u32[]{:S(2)}) copy-start(bf16[16,1,28,256]{3,2,0,1:T(8,128)(2,1)} %stack.109) | copy-start | bytes 688132
  64.5 14.6 %copy-start.17 = (bf16[16,1,28,256]{3,2,0,1:T(8,128)(2,1)S(1)}, bf16[16,1,28,256]{3,2,0,1:T(8,128)(2,1)}, u32[]{:S(2)}) copy-start(bf16[16,1,28,256]{3,2,0,1:T(8,128)(2,1)} %stack.110) | copy-start | bytes 688132
  119.8 5.1 copy-start.20
  119.8 5.8 copy-start.18
  353.1 5.4 copy-start.28
  353.1 5.4 copy-start.37
  353.2 18.2 %copy-start.7 = (bf16[256,1024]{1,0:T(8,128)(2,1)S(1)}, bf16[256,1024]{1,0:T(8,128)(2,1)}, u32[]{:S(2)}) copy-start(bf16[256,1024]{1,0:T(8,128)(2,1)} %copy-done.6) | copy-start | bytes 1572868
  353.3 6.8 collective-permute-start.4
  355.3 17.4 %copy-start.33 = (bf16[16,16,8,32]{3,1,2,0:T(8,128)(2,1)S(1)}, bf16[16,16,8,32]{3,1,2,0:T(8,128)(2,1)}, u32[]{:S(2)}) copy-start(bf16[16,16,8,32]{3,1,2,0:T(8,128)(2,1)} %fusion.20) | copy-start | bytes 393220
  355.3 8.5 %collective-permute-start.5 = (bf16[28,6,512]{2,0,1:T(8,128)(2,1)S(1)}, bf16[28,6,512]{2,0,1:T(8,128)(2,1)S(1)}, u32[]{:S(2)}, u32[]{:S(2)}) collective-permute-start(bf16[28,6,512]{2,0,1:T(8,128)(2,1)S(1)} %get-tuple-element.193), channel_id=1, source_target_pairs={{1,0},{2,1},{3,2},{4,3},{5,4},{6,5},{7,6},{8,7},{9,8},{10,9},{11,1... | collective-permute-start | bytes 516104 | tf_op jit(solution)/shard_map/ppermute | solution.py:22
  360.1 13.1 %copy-start.10 = (bf16[256,256]{1,0:T(8,128)(2,1)S(1)}, bf16[256,256]{1,0:T(8,128)(2,1)}, u32[]{:S(2)}) copy-start(bf16[256,256]{1,0:T(8,128)(2,1)} %copy-done.9) | copy-start | bytes 393220
  360.1 13.1 %copy-start.12 = (bf16[256,256]{1,0:T(8,128)(2,1)S(1)}, bf16[256,256]{1,0:T(8,128)(2,1)}, u32[]{:S(2)}) copy-start(bf16[256,256]{1,0:T(8,128)(2,1)} %copy-done.11) | copy-start | bytes 393220
  364.8 19.0 %collective-permute-start.6 = (bf16[6,40,512]{2,0,1:T(8,128)(2,1)}, bf16[6,40,512]{2,0,1:T(8,128)(2,1)S(1)}, u32[]{:S(2)}, u32[]{:S(2)}) collective-permute-start(bf16[6,40,512]{2,0,1:T(8,128)(2,1)} %get-tuple-element.190), channel_id=1, source_target_pairs={{0,32},{32,64},{64,96},{96,128},{128,160},{160,192},{192,224},{224... | collective-permute-start | bytes 737288 | tf_op jit(solution)/shard_map/ppermute | solution.py:21
  369.9 13.9 %collective-permute-start.7 = (bf16[6,40,512]{2,0,1:T(8,128)(2,1)}, bf16[6,40,512]{2,0,1:T(8,128)(2,1)S(1)}, u32[]{:S(2)}, u32[]{:S(2)}) collective-permute-start(bf16[6,40,512]{2,0,1:T(8,128)(2,1)} %get-tuple-element.191), channel_id=1, source_target_pairs={{32,0},{64,32},{96,64},{128,96},{160,128},{192,160},{224,192},{256... | collective-permute-start | bytes 737288 | tf_op jit(solution)/shard_map/ppermute | solution.py:22
  385.1 108.8 %copy-start.16 = (f32[256,256]{1,0:T(8,128)S(1)}, f32[256,256]{1,0:T(8,128)}, u32[]{:S(2)}) copy-start(f32[256,256]{1,0:T(8,128)} %copy-done.15) | copy-start | bytes 786436
  385.1 108.8 %copy-start.35 = (bf16[256,768]{1,0:T(8,128)(2,1)S(1)}, bf16[256,768]{1,0:T(8,128)(2,1)}, u32[]{:S(2)}) copy-start(bf16[256,768]{1,0:T(8,128)(2,1)} %param.35) | copy-start | bytes 1179652
  493.3 195.2 %copy-start.1 = (bf16[256,1024]{1,0:T(8,128)(2,1)S(1)}, bf16[256,1024]{1,0:T(8,128)(2,1)}, u32[]{:S(2)}) copy-start(bf16[256,1024]{1,0:T(8,128)(2,1)} %param.38) | copy-start | bytes 1572868
  681.6 6.0 copy-start.14
  (20 other events, 45.6 us)
Sparse Core Ops, SparseCore 0:
  386.8 294.7 all-reduce.6
where the time goes:
time: 707 us; the launch traced here: 696 us
  local copies, waits for them, and re-layouts  249 us (35%)
  waiting for transfers between devices  211 us (30%)
  blocking collectives  107 us (15%)
  matrix products  58.8 us (8%)
  other arithmetic  31.2 us (4%)
  starting transfers between devices  23.1 us (3%)
  between operations  15.2 us (2%)
    psum x1, waiting for transfers between devices, on_device(): lax.psum((local_qkv, local_proj, local_up, local_down, local_gain_attn, l...  187 us
    psum x1, blocking collectives, on_device(): lax.psum((local_qkv, local_proj, local_up, local_down, local_gain_attn, l...  107 us
    reshape x4, local copies, waits for them, and re-layouts, band_strips(): strips.reshape(rows, span * padded.shape[1], heads, padded.shape[2] // he...  80.1 us
    unnamed x112, local copies, waits for them, and re-layouts  33.7 us
    another operation x28, local copies, waits for them, and re-layouts, row_strips(): jnp.stack([lax.slice_in_dim(padded, offset, offset + rows, axis=0) for of...  29 us
    scatter-add x12, local copies, waits for them, and re-layouts, unstrip(): total = total.at[offset:offset + rows].add(strip_sum[:, offset])  25.4 us
    transpose x1, local copies, waits for them, and re-layouts, on_device(): jnp.einsum('ihcn,ichd->inhd', probs_bf, d_attended4, preferred_element_ty...  20.3 us
    transpose x1, local copies, waits for them, and re-layouts, on_device(): jnp.einsum('ihcn,ichd->inhd', d_scores, queries4, preferred_element_type=...  20.3 us
  transfers between devices with their start and end apart: 9, of which 6 were waited for; matrix products, arithmetic and copies ran while one was open for 1% of the time, Pallas kernels for 0%

commit v1 on v0

--- a/solution.py
+++ b/solution.py
@@ -181,8 +181,10 @@
     local_qkv = contract_rows(flat, d_projected)
     grad_frame = (d_mid + contract_cols(d_projected, weight_qkv)).astype(jnp.bfloat16)
     sum_qkv, sum_proj, sum_up, sum_down, sum_gain_attn, sum_gain_mlp = lax.psum(
-        (local_qkv, local_proj, local_up, local_down, local_gain_attn, local_gain_mlp),
-        ("lat", "lon"),
+        lax.psum(
+            (local_qkv, local_proj, local_up, local_down, local_gain_attn, local_gain_mlp), "lat"
+        ),
+        "lon",
     )
     return (
         block_out.reshape(lat_rows, lon_cols, width),

time: 707 us -> 851 us (1.20)
  the two profiles are of different devices: /device:TPU:17 before, /device:TPU:1 now
where the time goes in v1:
time: 851 us; the launch traced here: 839 us
  waiting for transfers between devices  351 us (41%)
  local copies, waits for them, and re-layouts  249 us (29%)
  blocking collectives  100 us (12%)
  matrix products  58.8 us (7%)
  starting transfers between devices  34 us (4%)
  other arithmetic  31.2 us (4%)
  between operations  15.2 us (2%)
    psum x1, waiting for transfers between devices, on_device(): lax.psum((local_qkv, local_proj, local_up, local_down, local_gain_attn, l...  187 us
    psum x1, waiting for transfers between devices, on_device(): lax.psum(lax.psum((local_qkv, local_proj, local_up, local_down, local_gai...  147 us
    reshape x4, local copies, waits for them, and re-layouts, band_strips(): strips.reshape(rows, span * padded.shape[1], heads, padded.shape[2] // he...  80.1 us
    psum x1, blocking collectives, on_device(): lax.psum(lax.psum((local_qkv, local_proj, local_up, local_down, local_gai...  69 us
    unnamed x112, local copies, waits for them, and re-layouts  33.7 us
    psum x1, blocking collectives, on_device(): lax.psum((local_qkv, local_proj, local_up, local_down, local_gain_attn, l...  31.1 us
    another operation x28, local copies, waits for them, and re-layouts, row_strips(): jnp.stack([lax.slice_in_dim(padded, offset, offset + rows, axis=0) for of...  29 us
    scatter-add x12, local copies, waits for them, and re-layouts, unstrip(): total = total.at[offset:offset + rows].add(strip_sum[:, offset])  25.4 us
  transfers between devices with their start and end apart: 10, of which 7 were waited for; matrix products, arithmetic and copies ran while one was open for 1% of the time, Pallas kernels for 0%

profile of v1, /device:TPU:1, one launch (start us, length us, event | category | flops | bytes accessed | tf_op | source)
XLA Modules:
  0.0 839.2 jit_solution(13527819728000456693)
XLA Ops:
  8.7 4.5 collective-permute-start
  13.2 6.2 collective-permute-start.1
  20.5 3.6 collective-permute-start.2
  26.7 5.3 collective-permute-done.3
  79.0 18.8 %copy.50 = bf16[16,13,28,256]{2,1,3,0:T(8,128)(2,1)} copy(bf16[16,13,28,256]{3,2,0,1:T(8,128)(2,1)} %constant_dynamic-update-slice_fusion.13) | data formatting | bytes 5963776 | tf_op jit(solution)/shard_map/reshape | solution.py:83
  97.9 21.2 %reshape.626 = bf16[16,364,8,32]{1,3,2,0:T(8,128)(2,1)} reshape(bf16[16,13,28,256]{2,1,3,0:T(8,128)(2,1)} %copy.50) | data formatting | bytes 5963776 | tf_op jit(solution)/shard_map/reshape | solution.py:83
  127.8 18.8 %copy.49 = bf16[16,13,28,256]{2,1,3,0:T(8,128)(2,1)} copy(bf16[16,13,28,256]{3,2,0,1:T(8,128)(2,1)} %constant_dynamic-update-slice_fusion) | data formatting | bytes 5963776 | tf_op jit(solution)/shard_map/reshape | solution.py:83
  146.6 21.2 %reshape.625 = bf16[16,364,8,32]{1,3,2,0:T(8,128)(2,1)} reshape(bf16[16,13,28,256]{2,1,3,0:T(8,128)(2,1)} %copy.49) | data formatting | bytes 5963776 | tf_op jit(solution)/shard_map/reshape | solution.py:83
  167.8 2.6 fusion.52
  170.5 3.8 fusion.78
  181.2 4.3 fusion.49
  185.5 17.5 %fusion.20 = bf16[16,16,8,32]{3,1,2,0:T(8,128)(2,1)} fusion(bf16[16,364,8,32]{1,3,2,0:T(8,128)(2,1)} %reshape.626, f32[16,8,16,364]{3,2,1,0:T(8,128)} %fusion.49, f32[16,8,16,364]{3,2,1,0:T(8,128)} %copy-done.5, f32[16,8,16]{2,1,0:T(8,128)S(1)} %get-tuple-element.232), kind=kOutput, calls=%fused_computation.27 | convolution fusion | flops 52996460 | bytes 9084928 | tf_op jit(solution)/shard_map/ihcn,inhd->ichd/dot_general | solution.py:161
  203.0 17.6 %convolution_bitcast_fusion.1 = f32[16,364,8,32]{1,3,2,0:T(8,128)} fusion(f32[16,8,16,364]{3,2,1,0:T(8,128)} %fusion.49, bf16[16,16,8,32]{3,2,1,0:T(8,128)(2,1)S(1)} %reshape.602, f32[16,8,16,364]{3,2,1,0:T(8,128)} %copy-done.5, f32[16,8,16]{2,1,0:T(8,128)S(1)} %get-tuple-element.232), kind=kOutput, calls=%fused_computation.8 | convolution fusion | flops 52930924 | bytes 12066816 | tf_op jit(solution)/shard_map/ihcn,ichd->inhd/dot_general | solution.py:164
  220.6 5.6 convolution_bitcast_fusion
  226.2 20.3 %copy.46 = f32[16,364,8,32]{3,2,0,1:T(8,128)} copy(f32[16,364,8,32]{1,3,2,0:T(8,128)} %convolution_bitcast_fusion) | data formatting | bytes 11927552 | tf_op jit(solution)/shard_map/ihcn,ichd->inhd/transpose | solution.py:167
  246.5 16.9 %reshape.609 = f32[16,13,28,256]{3,0,2,1:T(8,128)} reshape(f32[16,364,8,32]{3,2,0,1:T(8,128)} %copy.46) | data formatting | bytes 11927552 | tf_op jit(solution)/shard_map/reshape | solution.py:169
  263.4 20.3 %copy.44 = f32[16,364,8,32]{3,2,0,1:T(8,128)} copy(f32[16,364,8,32]{1,3,2,0:T(8,128)} %convolution_bitcast_fusion.1) | data formatting | bytes 11927552 | tf_op jit(solution)/shard_map/ihcn,ichd->inhd/transpose | solution.py:164
  283.8 16.8 %reshape.608 = f32[16,13,28,256]{3,0,2,1:T(8,128)} reshape(f32[16,364,8,32]{3,2,0,1:T(8,128)} %copy.44) | data formatting | bytes 11927552 | tf_op jit(solution)/shard_map/reshape | solution.py:166
  300.6 3.8 constant_dynamic-update-slice_fusion.27
  307.0 4.1 copy-done.2
  338.1 2.5 scatter-add.59
  342.0 2.5 scatter-add.60
  345.9 2.5 scatter-add.61
  349.8 2.5 scatter-add.64
  352.5 3.1 collective-permute-start.4
  355.7 5.2 collective-permute-start.5
  363.7 8.5 %collective-permute-start.6 = (bf16[6,40,512]{2,0,1:T(8,128)(2,1)}, bf16[6,40,512]{2,0,1:T(8,128)(2,1)S(1)}, u32[]{:S(2)}, u32[]{:S(2)}) collective-permute-start(bf16[6,40,512]{2,0,1:T(8,128)(2,1)} %get-tuple-element.196), channel_id=1, source_target_pairs={{0,32},{32,64},{64,96},{96,128},{128,160},{160,192},{192,224},{224... | collective-permute-start | bytes 737288 | tf_op jit(solution)/shard_map/ppermute | solution.py:21
  376.5 9.6 %collective-permute-done.6 = bf16[6,40,512]{2,0,1:T(8,128)(2,1)S(1)} collective-permute-done((bf16[6,40,512]{2,0,1:T(8,128)(2,1)}, bf16[6,40,512]{2,0,1:T(8,128)(2,1)S(1)}, u32[]{:S(2)}, u32[]{:S(2)}) %collective-permute-start.6) | collective-permute-done | bytes 245792 | tf_op jit(solution)/shard_map/ppermute | solution.py:21
  389.1 187.2 %all-reduce.12.cloned.1.call-done = (f32[256,768]{0,1:T(8,128)}, f32[256,256]{1,0:T(8,128)}, f32[256,1024]{1,0:T(8,128)}, f32[1024,256]{1,0:T(8,128)}) async-done(((f32[256,768]{0,1:T(8,128)}, f32[256,256]{1,0:T(8,128)}, f32[256,1024]{1,0:T(8,128)}, f32[1024,256]{1,0:T(8,128)}), (f32[256,768]{0,1:T(8,128)}, f32[256,256]{1,0:T(8,128)}, f32[256,1024]{1,0:T(8,128)}, ...) | async-done | bytes 3145744 | tf_op jit(solution)/shard_map/psum | solution.py:184
  576.3 31.1 %all-reduce.5 = (f32[256]{0:T(256)S(1)}, f32[256]{0:T(256)S(1)}) all-reduce(f32[256]{0:T(256)S(1)} %get-tuple-element.180, f32[256]{0:T(256)S(1)} %get-tuple-element.182), channel_id=1, replica_groups=mesh['lat'=16,'lon'=32] {'lat'}, use_global_device_ids=true, to_apply=%region_16.17 | all-reduce | flops 512 | bytes 4096 | tf_op jit(solution)/shard_map/psum | solution.py:184
  607.4 69.0 %all-reduce.3 = (f32[256]{0:T(256)S(1)}, f32[256]{0:T(256)S(1)}) all-reduce(f32[256]{0:T(256)S(1)} %get-tuple-element.190, f32[256]{0:T(256)S(1)} %get-tuple-element.191), channel_id=1, replica_groups=mesh['lat'=16,'lon'=32] {'lon'}, use_global_device_ids=true, to_apply=%region_17.18 | all-reduce | flops 512 | bytes 4096 | tf_op jit(solution)/shard_map/psum | solution.py:183
  678.0 147.3 %all-reduce.10.cloned.1.call-done = (f32[256,768]{0,1:T(8,128)}, f32[256,256]{1,0:T(8,128)}, f32[256,1024]{1,0:T(8,128)}, f32[1024,256]{1,0:T(8,128)}) async-done(((f32[256,768]{0,1:T(8,128)}, f32[256,256]{1,0:T(8,128)}, f32[256,1024]{1,0:T(8,128)}, f32[1024,256]{1,0:T(8,128)}), (f32[256,768]{0,1:T(8,128)}, f32[256,256]{1,0:T(8,128)}, f32[256,1024]{1,0:T(8,128)}, ...) | async-done | bytes 3145744 | tf_op jit(solution)/shard_map/psum | solution.py:183
  (230 shorter events, 119.8 us)
Async XLA Ops:
  7.2 169.7 %copy-start = (bf16[256,1024]{1,0:T(8,128)(2,1)S(1)}, bf16[256,1024]{1,0:T(8,128)(2,1)}, u32[]{:S(2)}) copy-start(bf16[256,1024]{1,0:T(8,128)(2,1)} %param.38) | copy-start | bytes 1572868
  7.2 569.1 %all-reduce.12.cloned.1.call-start = ((), (), s32[]{:S(2)}) async-start(), calls=%async_computation.1 | async-start | bytes 6291456 | tf_op jit(solution)/shard_map/psum | solution.py:184
  8.7 11.4 %collective-permute-start = (bf16[16,6,512]{2,1,0:T(8,128)(2,1)S(1)}, bf16[16,6,512]{2,1,0:T(8,128)(2,1)S(1)}, u32[]{:S(2)}, u32[]{:S(2)}) collective-permute-start(bf16[16,6,512]{2,1,0:T(8,128)(2,1)S(1)} %get-tuple-element.230), channel_id=1, source_target_pairs={{0,1},{1,2},{2,3},{3,4},{4,5},{5,6},{6,7},{7,8},{8,9},{9,10},{10,1... | collective-permute-start | bytes 294920 | tf_op jit(solution)/shard_map/ppermute | solution.py:21
  13.2 7.1 collective-permute-start.1
  20.5 6.2 collective-permute-start.2
  24.1 7.9 collective-permute-start.3
  37.4 19.4 %copy-start.31 = (bf16[448,256]{1,0:T(8,128)(2,1)S(1)}, bf16[448,256]{1,0:T(8,128)(2,1)}, u32[]{:S(2)}) copy-start(bf16[448,256]{1,0:T(8,128)(2,1)} %get-tuple-element.212) | copy-start | bytes 688132
  37.4 20.1 %copy-start.30 = (bf16[448,256]{1,0:T(8,128)(2,1)S(1)}, bf16[448,256]{1,0:T(8,128)(2,1)}, u32[]{:S(2)}) copy-start(bf16[448,256]{1,0:T(8,128)(2,1)} %get-tuple-element.213) | copy-start | bytes 688132
  38.1 19.4 %copy-start.29 = (bf16[448,256]{1,0:T(8,128)(2,1)S(1)}, bf16[448,256]{1,0:T(8,128)(2,1)}, u32[]{:S(2)}) copy-start(bf16[448,256]{1,0:T(8,128)(2,1)} %get-tuple-element.214) | copy-start | bytes 688132
  63.7 10.2 %copy-start.26 = (bf16[16,1,28,256]{3,2,0,1:T(8,128)(2,1)S(1)}, bf16[16,1,28,256]{3,2,0,1:T(8,128)(2,1)}, u32[]{:S(2)}) copy-start(bf16[16,1,28,256]{3,2,0,1:T(8,128)(2,1)} %stack.104) | copy-start | bytes 688132
  63.7 10.9 %copy-start.25 = (bf16[16,1,28,256]{3,2,0,1:T(8,128)(2,1)S(1)}, bf16[16,1,28,256]{3,2,0,1:T(8,128)(2,1)}, u32[]{:S(2)}) copy-start(bf16[16,1,28,256]{3,2,0,1:T(8,128)(2,1)} %stack.105) | copy-start | bytes 688132
  63.7 11.7 %copy-start.24 = (bf16[16,1,28,256]{3,2,0,1:T(8,128)(2,1)S(1)}, bf16[16,1,28,256]{3,2,0,1:T(8,128)(2,1)}, u32[]{:S(2)}) copy-start(bf16[16,1,28,256]{3,2,0,1:T(8,128)(2,1)} %stack.106) | copy-start | bytes 688132
  63.7 12.4 %copy-start.23 = (bf16[16,1,28,256]{3,2,0,1:T(8,128)(2,1)S(1)}, bf16[16,1,28,256]{3,2,0,1:T(8,128)(2,1)}, u32[]{:S(2)}) copy-start(bf16[16,1,28,256]{3,2,0,1:T(8,128)(2,1)} %stack.107) | copy-start | bytes 688132
  63.7 13.1 %copy-start.21 = (bf16[16,1,28,256]{3,2,0,1:T(8,128)(2,1)S(1)}, bf16[16,1,28,256]{3,2,0,1:T(8,128)(2,1)}, u32[]{:S(2)}) copy-start(bf16[16,1,28,256]{3,2,0,1:T(8,128)(2,1)} %stack.108) | copy-start | bytes 688132
  63.7 13.9 %copy-start.19 = (bf16[16,1,28,256]{3,2,0,1:T(8,128)(2,1)S(1)}, bf16[16,1,28,256]{3,2,0,1:T(8,128)(2,1)}, u32[]{:S(2)}) copy-start(bf16[16,1,28,256]{3,2,0,1:T(8,128)(2,1)} %stack.109) | copy-start | bytes 688132
  63.7 14.6 %copy-start.17 = (bf16[16,1,28,256]{3,2,0,1:T(8,128)(2,1)S(1)}, bf16[16,1,28,256]{3,2,0,1:T(8,128)(2,1)}, u32[]{:S(2)}) copy-start(bf16[16,1,28,256]{3,2,0,1:T(8,128)(2,1)} %stack.110) | copy-start | bytes 688132
  119.1 5.8 copy-start.18
  352.3 8.5 %copy-start.28 = (f32[256,1024]{1,0:T(8,128)S(1)}, f32[256,1024]{1,0:T(8,128)}, u32[]{:S(2)}) copy-start(f32[256,1024]{1,0:T(8,128)} %copy-done.27) | copy-start | bytes 3145732
  352.3 8.5 %copy-start.37 = (bf16[256,256]{1,0:T(8,128)(2,1)S(1)}, bf16[256,256]{1,0:T(8,128)(2,1)}, u32[]{:S(2)}) copy-start(bf16[256,256]{1,0:T(8,128)(2,1)} %copy-done.36) | copy-start | bytes 393220
  352.5 21.3 %copy-start.7 = (bf16[256,1024]{1,0:T(8,128)(2,1)S(1)}, bf16[256,1024]{1,0:T(8,128)(2,1)}, u32[]{:S(2)}) copy-start(bf16[256,1024]{1,0:T(8,128)(2,1)} %copy-done.6) | copy-start | bytes 1572868
  352.5 9.9 %collective-permute-start.4 = (bf16[28,6,512]{2,0,1:T(8,128)(2,1)S(1)}, bf16[28,6,512]{2,0,1:T(8,128)(2,1)S(1)}, u32[]{:S(2)}, u32[]{:S(2)}) collective-permute-start(bf16[28,6,512]{2,0,1:T(8,128)(2,1)S(1)} %get-tuple-element.198), channel_id=1, source_target_pairs={{0,1},{1,2},{2,3},{3,4},{4,5},{5,6},{6,7},{7,8},{8,9},{9,10},{10,1... | collective-permute-start | bytes 516104 | tf_op jit(solution)/shard_map/ppermute | solution.py:21
  355.7 19.4 %copy-start.33 = (bf16[16,16,8,32]{3,1,2,0:T(8,128)(2,1)S(1)}, bf16[16,16,8,32]{3,1,2,0:T(8,128)(2,1)}, u32[]{:S(2)}) copy-start(bf16[16,16,8,32]{3,1,2,0:T(8,128)(2,1)} %fusion.20) | copy-start | bytes 393220
  355.7 7.1 collective-permute-start.5
  362.4 13.1 %copy-start.10 = (bf16[256,256]{1,0:T(8,128)(2,1)S(1)}, bf16[256,256]{1,0:T(8,128)(2,1)}, u32[]{:S(2)}) copy-start(bf16[256,256]{1,0:T(8,128)(2,1)} %copy-done.9) | copy-start | bytes 393220
  362.4 13.1 %copy-start.12 = (bf16[256,256]{1,0:T(8,128)(2,1)S(1)}, bf16[256,256]{1,0:T(8,128)(2,1)}, u32[]{:S(2)}) copy-start(bf16[256,256]{1,0:T(8,128)(2,1)} %copy-done.11) | copy-start | bytes 393220
  363.7 22.4 %collective-permute-start.6 = (bf16[6,40,512]{2,0,1:T(8,128)(2,1)}, bf16[6,40,512]{2,0,1:T(8,128)(2,1)S(1)}, u32[]{:S(2)}, u32[]{:S(2)}) collective-permute-start(bf16[6,40,512]{2,0,1:T(8,128)(2,1)} %get-tuple-element.196), channel_id=1, source_target_pairs={{0,32},{32,64},{64,96},{96,128},{128,160},{160,192},{192,224},{224... | collective-permute-start | bytes 737288 | tf_op jit(solution)/shard_map/ppermute | solution.py:21
  372.2 13.9 %collective-permute-start.7 = (bf16[6,40,512]{2,0,1:T(8,128)(2,1)}, bf16[6,40,512]{2,0,1:T(8,128)(2,1)S(1)}, u32[]{:S(2)}, u32[]{:S(2)}) collective-permute-start(bf16[6,40,512]{2,0,1:T(8,128)(2,1)} %get-tuple-element.197), channel_id=1, source_target_pairs={{32,0},{64,32},{96,64},{128,96},{160,128},{192,160},{224,192},{256... | collective-permute-start | bytes 737288 | tf_op jit(solution)/shard_map/ppermute | solution.py:22
  389.0 288.0 %copy-start.16 = (f32[256,256]{1,0:T(8,128)S(1)}, f32[256,256]{1,0:T(8,128)}, u32[]{:S(2)}) copy-start(f32[256,256]{1,0:T(8,128)} %copy-done.15) | copy-start | bytes 786436
  389.0 288.0 %copy-start.35 = (bf16[256,768]{1,0:T(8,128)(2,1)S(1)}, bf16[256,768]{1,0:T(8,128)(2,1)}, u32[]{:S(2)}) copy-start(bf16[256,768]{1,0:T(8,128)(2,1)} %param.35) | copy-start | bytes 1179652
  389.0 436.3 %all-reduce.10.cloned.1.call-start = ((), (), s32[]{:S(2)}) async-start(), calls=%async_computation | async-start | bytes 6291456 | tf_op jit(solution)/shard_map/psum | solution.py:183
  676.5 155.7 %copy-start.1 = (bf16[256,1024]{1,0:T(8,128)(2,1)S(1)}, bf16[256,1024]{1,0:T(8,128)(2,1)}, u32[]{:S(2)}) copy-start(bf16[256,1024]{1,0:T(8,128)(2,1)} %param.38) | copy-start | bytes 1572868
  825.3 6.0 copy-start.14
  (21 other events, 50.7 us)
Sparse Core Ops, SparseCore 0:
  389.2 187.0 all-reduce.11
  579.5 245.7 all-reduce.9
